TPU v7x, 512 devices: a whole 4x8x8 slice. The times are simulated.
512 devices in a mesh: expert: 64 (over y, x, core), hidden: 8 (over z).
Axes of the slice: x: 4, y: 8, z: 8, core: 2. Of those that a mesh axis runs over, the one named last changes fastest.
Arguments:
- tokens: bfloat16 [4096, 4096], P('expert', 'hidden'), may hold values from -6 to 6
- expert_ids: int32 [4096, 8], P('expert'), may hold values from 0 to 63, all different within a row; in each aligned block of 64 rows (0 to 63, 64 to 127, ...) at most 16 rows name the same one
- gate_weights: float32 [4096, 8], P('expert'), may hold values from 0.05 to 0.5
- gate_proj: bfloat16 [64, 1536, 4096], P('expert', 'hidden'), may hold values from -0.09375 to 0.09375
- up_proj: bfloat16 [64, 1536, 4096], P('expert', 'hidden'), may hold values from -0.09375 to 0.09375
- down_proj: bfloat16 [64, 1536, 4096], P('expert', None, 'hidden'), may hold values from -0.15625 to 0.15625
Outputs:
- moe_out: bfloat16 [4096, 4096], P('expert', 'hidden')
Inputs may be any that keep to these rules, and one draw needn't show every extreme that they name: `expert_ids`: each row names 8 different experts; in each aligned block of 64 rows no expert is named by more than 16 rows.
All inputs are finite; a program needn't handle non-finite values.
Results may differ from a plain program's by a relative error of at most 0.0057.
Values may be sent and summed in bfloat16 or wider, within the bound.
No kernel may reach another device: no remote copies, remote signals or barrier semaphores. Data moves between devices by JAX's collectives and lax.ppermute only.
A program may use at most 64 MiB of HBM per device.

v0:
```python
import jax
import jax.numpy as jnp
from jax import lax
from jax.sharding import PartitionSpec as P


def on_device(tokens, expert_ids, gate_weights, gate_proj, up_proj, down_proj):
    local_count = gate_proj.shape[0]
    experts_all = local_count * lax.axis_size("expert")
    tok_rows = tokens.shape[0]
    top_count = expert_ids.shape[1]
    capacity = 2 * tok_rows * top_count // experts_all
    flat_ids = expert_ids.reshape(-1)
    onehot = (flat_ids[:, None] == jnp.arange(experts_all, dtype=jnp.int32)[None, :]).astype(
        jnp.int32
    )
    slot_index = jnp.sum((jnp.cumsum(onehot, axis=0) - onehot) * onehot, axis=1)
    position = flat_ids * capacity + slot_index
    token_of = jnp.arange(tok_rows * top_count, dtype=jnp.int32) // top_count
    full_rows = lax.all_gather(tokens, "hidden", axis=1, tiled=True)
    packed = jnp.zeros((experts_all * capacity, full_rows.shape[1]), full_rows.dtype)
    packed = packed.at[position].set(full_rows[token_of])
    arrived = lax.all_to_all(
        packed.reshape(experts_all, capacity, full_rows.shape[1]),
        "expert",
        split_axis=0,
        concat_axis=1,
        tiled=True,
    )
    gate_sum = jnp.einsum("lrd,lfd->lfr", arrived, gate_proj, preferred_element_type=jnp.float32)
    up_sum = jnp.einsum("lrd,lfd->lfr", arrived, up_proj, preferred_element_type=jnp.float32)
    activation = (jax.nn.silu(gate_sum) * up_sum).astype(jnp.bfloat16)
    expert_out = jnp.einsum(
        "lfr,lfd->lrd",
        lax.all_gather(activation, "hidden", axis=1, tiled=True),
        down_proj,
        preferred_element_type=jnp.float32,
    ).astype(jnp.bfloat16)
    returned = lax.all_to_all(expert_out, "expert", split_axis=1, concat_axis=0, tiled=True)
    gathered = returned.reshape(experts_all * capacity, returned.shape[2])[position]
    gathered = gathered.reshape(tok_rows, top_count, returned.shape[2]).astype(jnp.float32)
    mixed = jnp.sum(gathered * gate_weights[:, :, None], axis=1)
    return mixed.astype(jnp.bfloat16)


def solution(mesh):
    in_specs = (
        P("expert", "hidden"),
        P("expert", None),
        P("expert", None),
        P("expert", "hidden", None),
        P("expert", "hidden", None),
        P("expert", None, "hidden"),
    )
    out_specs = P("expert", "hidden")
    return jax.shard_map(
        on_device, mesh=mesh, in_specs=in_specs, out_specs=out_specs, check_vma=False
    )
```

profile of v0, /device:TPU:1, one launch (start us, length us, event | category | flops | bytes accessed | tf_op | source)
XLA Modules:
  0.0 375.7 jit_solution(17025929349063810798)
XLA Ops:
  6.5 0.9 copy.20
  7.6 0.7 broadcast_multiply_fusion
  8.3 1.2 reduce-window.6
  9.5 0.2 slice_reduce_fusion
  9.9 0.1 mul.38
  10.0 27.1 %all_gather.6 = bf16[64,4096]{1,0:T(8,128)(2,1)S(1)} all-gather(bf16[64,512]{1,0:T(8,128)(2,1)} %param.6), channel_id=1, replica_groups=mesh['expert'=64,'hidden'=8] {'hidden'}, dimensions={1}, use_global_device_ids=true | all-gather | bytes 589824 | tf_op jit(solution)/shard_map/all_gather | solution.py:20
  37.1 0.1 fusion.29
  37.3 4.4 %gather_fusion = bf16[512,4096]{1,0:T(8,128)(2,1)} fusion(bf16[64,4096]{1,0:T(8,128)(2,1)S(1)} %all_gather.6, s32[1024]{0:T(1024)S(1)} %pad_clamp_fusion.1), kind=kCustom, calls=%fused_computation | custom fusion | bytes 8390656 | tf_op jit(solution)/shard_map/gather | solution.py:22
  41.6 12.4 %scatter_custom_fusion = bf16[1024,4096]{1,0:T(8,128)(2,1)} fusion(s32[512]{0:T(512)S(1)} %bitcast.75, bf16[512,4096]{1,0:T(8,128)(2,1)} %gather_fusion, bf16[]{:T(256)} %constant.26.clone.1), kind=kCustom, calls=%fused_computation.3 | custom fusion | bytes 8389120 | tf_op jit(solution)/shard_map/scatter | solution.py:22
  54.1 201.0 %all_to_all.8 = bf16[64,16,4096]{2,1,0:T(8,128)(2,1)S(1)} all-to-all(bf16[64,16,4096]{2,1,0:T(8,128)(2,1)} %bitcast.68), channel_id=1, replica_groups=mesh['expert'=64,'hidden'=8] {'expert'}, dimensions={0} | all-to-all | bytes 16777216 | tf_op jit(solution)/shard_map/all_to_all | solution.py:23
  255.0 2.9 fusion.14
  258.0 3.7 fusion.23
  261.7 43.4 %all-gather.3.cloned.1.call-done = bf16[1536,1024]{1,0:T(8,128)(2,1)} async-done(((bf16[192,1024]{1,0:T(8,128)(2,1)}), bf16[1536,1024]{1,0:T(8,128)(2,1)}) %all-gather.3.cloned.1.call-update) | async-done | bytes 3145744 | tf_op jit(solution)/shard_map/all_gather | solution.py:35
  305.1 3.7 fusion.11
  308.8 3.0 copy.31
  311.8 0.5 broadcast.125
  312.3 8.3 %reduce.2 = bf16[1024,512]{1,0:T(8,128)(2,1)S(1)} reduce(bf16[1024,1,512]{2,1,0:T(2,128)(2,1)} %bitcast.73, bf16[]{:T(256)} %broadcast.125), dimensions={1}, to_apply=%bitcast.67.reduce_sub_computation | reduce | bytes 2097154
  320.6 1.6 reshape.173
  322.2 10.3 %all-to-all-start.1 = ((bf16[64,2,4096]{2,1,0:T(2,128)(2,1)}), bf16[64,2,4096]{2,1,0:T(2,128)(2,1)S(1)}, u32[]{:S(2)}, u32[]{:S(2)}) async-start(bf16[64,2,4096]{2,1,0:T(2,128)(2,1)} %reshape.173), calls=%async_computation.1 | async-start | bytes 2097152 | tf_op jit(solution)/shard_map/all_to_all | solution.py:39
  332.6 27.9 %all-to-all-done.1 = bf16[64,2,4096]{2,1,0:T(2,128)(2,1)S(1)} async-done(((bf16[64,2,4096]{2,1,0:T(2,128)(2,1)}), bf16[64,2,4096]{2,1,0:T(2,128)(2,1)S(1)}, u32[]{:S(2)}, u32[]{:S(2)}) %all-to-all-start.1) | async-done | bytes 1048608 | tf_op jit(solution)/shard_map/all_to_all | solution.py:39
  360.5 3.5 reshape.174
  364.0 1.9 copy.30
  365.9 2.0 gather_fusion.1
  367.8 1.0 fusion.26
  (21 shorter events, 0.5 us)
Async XLA Ops:
  6.5 298.6 %copy-start = (bf16[1,1536,512]{2,1,0:T(8,128)(2,1)S(1)}, bf16[1,1536,512]{2,1,0:T(8,128)(2,1)}, u32[]{:S(2)}) copy-start(bf16[1,1536,512]{2,1,0:T(8,128)(2,1)} %param.11) | copy-start | bytes 4718596
  6.5 298.6 %all-gather.3.cloned.1.call-start = ((), (), s32[]{:S(2)}) async-start(), calls=%async_computation.2 | async-start | bytes 3538944 | tf_op jit(solution)/shard_map/all_gather | solution.py:35
  54.1 201.0 %copy-start.2 = (bf16[1,192,4096]{2,1,0:T(8,128)(2,1)S(1)}, bf16[1,192,4096]{2,1,0:T(8,128)(2,1)}, u32[]{:S(2)}) copy-start(bf16[1,192,4096]{2,1,0:T(8,128)(2,1)} %param.9) | copy-start | bytes 4718596
  255.0 2.9 copy-start.3
  311.8 20.7 %copy-start.1 = (f32[64,8]{0,1:T(8,128)S(1)}, f32[64,8]{0,1:T(8,128)}, u32[]{:S(2)}) copy-start(f32[64,8]{0,1:T(8,128)} %param.8) | copy-start | bytes 6148
  322.2 38.3 %all-to-all-start.1 = ((bf16[64,2,4096]{2,1,0:T(2,128)(2,1)}), bf16[64,2,4096]{2,1,0:T(2,128)(2,1)S(1)}, u32[]{:S(2)}, u32[]{:S(2)}) async-start(bf16[64,2,4096]{2,1,0:T(2,128)(2,1)} %reshape.173), calls=%async_computation.1 | async-start | bytes 2097152 | tf_op jit(solution)/shard_map/all_to_all | solution.py:39
Sparse Core Ops, SparseCore 0:
  261.8 43.2 all-gather.2
where the time goes:
time: 376 us
  blocking collectives  228 us (61%)
  waiting for transfers between devices  71.3 us (19%)
  local copies, waits for them, and re-layouts  30.8 us (8%)
  between operations  13.5 us (4%)
  other arithmetic  11.3 us (3%)
  starting transfers between devices  10.4 us (3%)
  matrix products  10.3 us (3%)
    all_to_all x1, blocking collectives, on_device(): lax.all_to_all(packed.reshape(experts_all, capacity, full_rows.shape[1]),...  201 us
    all_gather x1, waiting for transfers between devices, on_device(): lax.all_gather(activation, 'hidden', axis=1, tiled=True)  43.4 us
    all_to_all x1, waiting for transfers between devices, on_device(): lax.all_to_all(expert_out, 'expert', split_axis=1, concat_axis=0, tiled=T...  27.9 us
    all_gather x1, blocking collectives, on_device(): full_rows = lax.all_gather(tokens, 'hidden', axis=1, tiled=True)  27.1 us
    scatter x1, local copies, waits for them, and re-layouts, on_device(): packed = packed.at[position].set(full_rows[token_of])  12.4 us
    all_to_all x1, starting transfers between devices, on_device(): lax.all_to_all(expert_out, 'expert', split_axis=1, concat_axis=0, tiled=T...  10.3 us
    unnamed x14, local copies, waits for them, and re-layouts  8.43 us
    unnamed x1, other arithmetic  8.25 us
  transfers between devices with their start and end apart: 2, of which 2 were waited for; matrix products, arithmetic and copies ran while one was open for 0% of the time, Pallas kernels for 0%

commit v1 on v0

--- a/solution.py
+++ b/solution.py
@@ -2,6 +2,18 @@
 import jax.numpy as jnp
 from jax import lax
 from jax.sharding import PartitionSpec as P
+
+
+def product_in_turn(array, axis, dim, contribution):
+    length, position = (lax.axis_size(axis), lax.axis_index(axis))
+    behind = [(i, (i - 1) % length) for i in range(length)]
+    rows = array.shape[dim]
+    current = array
+    total = contribution(current, position * rows)
+    for step in range(1, length):
+        current = lax.ppermute(current, axis, behind)
+        total = total + contribution(current, (position + step) % length * rows)
+    return total
 
 
 def on_device(tokens, expert_ids, gate_weights, gate_proj, up_proj, down_proj):
@@ -30,11 +42,16 @@
     gate_sum = jnp.einsum("lrd,lfd->lfr", arrived, gate_proj, preferred_element_type=jnp.float32)
     up_sum = jnp.einsum("lrd,lfd->lfr", arrived, up_proj, preferred_element_type=jnp.float32)
     activation = (jax.nn.silu(gate_sum) * up_sum).astype(jnp.bfloat16)
-    expert_out = jnp.einsum(
-        "lfr,lfd->lrd",
-        lax.all_gather(activation, "hidden", axis=1, tiled=True),
-        down_proj,
-        preferred_element_type=jnp.float32,
+    expert_out = product_in_turn(
+        activation,
+        "hidden",
+        1,
+        lambda part, start: jnp.einsum(
+            "lfr,lfd->lrd",
+            part,
+            lax.dynamic_slice_in_dim(down_proj, start, part.shape[1], axis=1),
+            preferred_element_type=jnp.float32,
+        ),
     ).astype(jnp.bfloat16)
     returned = lax.all_to_all(expert_out, "expert", split_axis=1, concat_axis=0, tiled=True)
     gathered = returned.reshape(experts_all * capacity, returned.shape[2])[position]

time: 376 us -> 398 us (1.059)
  starting transfers between devices: 10.4 us -> 53.8 us
  between operations: 13.5 us -> 0.29 us
  waiting for transfers between devices: 71.3 us -> 62.8 us
    all_gather x1 -> x0, waiting for transfers between devices: 43.4 us -> none  [on_device(): lax.all_gather(activation, 'hidden', axis=1, tiled=True)]
    ppermute x0 -> x7, starting transfers between devices: none -> 35.5 us  [product_in_turn(): current = lax.ppermute(current, axis, behind)]
    ppermute x0 -> x7, waiting for transfers between devices: none -> 34.9 us  [product_in_turn(): current = lax.ppermute(current, axis, behind)]
    all_to_all x1, starting transfers between devices: 10.3 us -> 18.3 us  [on_device(): lax.all_to_all(expert_out, 'expert', split_axis=1, concat_axis=0, tiled=T...]
  transfers between devices with their start and end apart: 2 -> 8, of which waited for: 2 -> 8; matrix products, arithmetic and copies ran while one was open for 0% -> 1% of each run, Pallas kernels for 0% -> 0%
where the time goes in v1:
time: 398 us; the launch traced here: 397 us
  blocking collectives  228 us (57%)
  waiting for transfers between devices  62.8 us (16%)
  starting transfers between devices  53.8 us (14%)
  local copies, waits for them, and re-layouts  30.6 us (8%)
  other arithmetic  11.2 us (3%)
  matrix products  10 us (3%)
    all_to_all x1, blocking collectives, on_device(): lax.all_to_all(packed.reshape(experts_all, capacity, full_rows.shape[1]),...  201 us
    ppermute x7, starting transfers between devices, product_in_turn(): current = lax.ppermute(current, axis, behind)  35.5 us
    ppermute x7, waiting for transfers between devices, product_in_turn(): current = lax.ppermute(current, axis, behind)  34.9 us
    all_to_all x1, waiting for transfers between devices, on_device(): lax.all_to_all(expert_out, 'expert', split_axis=1, concat_axis=0, tiled=T...  27.9 us
    all_gather x1, blocking collectives, on_device(): full_rows = lax.all_gather(tokens, 'hidden', axis=1, tiled=True)  27.1 us
    all_to_all x1, starting transfers between devices, on_device(): lax.all_to_all(expert_out, 'expert', split_axis=1, concat_axis=0, tiled=T...  18.3 us
    scatter x1, local copies, waits for them, and re-layouts, on_device(): packed = packed.at[position].set(full_rows[token_of])  12.4 us
    unnamed x14, local copies, waits for them, and re-layouts  8.31 us
  transfers between devices with their start and end apart: 8, of which 8 were waited for; matrix products, arithmetic and copies ran while one was open for 1% of the time, Pallas kernels for 0%

profile of v1, /device:TPU:1, one launch (start us, length us, event | category | flops | bytes accessed | tf_op | source)
XLA Modules:
  0.0 397.1 jit_solution(5548831401026045196)
XLA Ops:
  3.5 27.1 %all_gather.3 = bf16[64,4096]{1,0:T(8,128)(2,1)S(1)} all-gather(bf16[64,512]{1,0:T(8,128)(2,1)} %param.6), channel_id=1, replica_groups=mesh['expert'=64,'hidden'=8] {'hidden'}, dimensions={1}, use_global_device_ids=true | all-gather | bytes 589824 | tf_op jit(solution)/shard_map/all_gather | solution.py:32
  30.7 4.4 %gather_fusion = bf16[512,4096]{1,0:T(8,128)(2,1)} fusion(bf16[64,4096]{1,0:T(8,128)(2,1)S(1)} %all_gather.3, s32[1024]{0:T(1024)S(1)} %pad_clamp_fusion.1), kind=kCustom, calls=%fused_computation | custom fusion | bytes 8390656 | tf_op jit(solution)/shard_map/gather | solution.py:34
  35.1 12.4 %scatter_custom_fusion = bf16[1024,4096]{1,0:T(8,128)(2,1)} fusion(s32[512]{0:T(512)S(1)} %bitcast.115, bf16[512,4096]{1,0:T(8,128)(2,1)} %gather_fusion, bf16[]{:T(256)} %constant.71.clone.1), kind=kCustom, calls=%fused_computation.3 | custom fusion | bytes 8389120 | tf_op jit(solution)/shard_map/scatter | solution.py:34
  47.5 201.1 %all_to_all.8 = bf16[64,16,4096]{2,1,0:T(8,128)(2,1)S(1)} all-to-all(bf16[64,16,4096]{2,1,0:T(8,128)(2,1)} %bitcast.107), channel_id=1, replica_groups=mesh['expert'=64,'hidden'=8] {'expert'}, dimensions={0} | all-to-all | bytes 16777216 | tf_op jit(solution)/shard_map/all_to_all | solution.py:35
  251.6 2.9 fusion.16
  254.5 4.6 %collective-permute-start = (bf16[1,192,1024]{2,1,0:T(8,128)(2,1)S(1)}, bf16[1,192,1024]{2,1,0:T(8,128)(2,1)S(1)}, u32[]{:S(2)}, u32[]{:S(2)}) collective-permute-start(bf16[1,192,1024]{2,1,0:T(8,128)(2,1)S(1)} %bitcast.113), channel_id=1, source_target_pairs={{0,7},{1,0},{2,1},{3,2},{4,3},{5,4},{6,5},{7,6},{8,15},{9,8},{10,9... | collective-permute-start | bytes 1179656 | tf_op jit(solution)/shard_map/ppermute | solution.py:14
  259.2 6.2 %collective-permute-done = bf16[1,192,1024]{2,1,0:T(8,128)(2,1)S(1)} collective-permute-done((bf16[1,192,1024]{2,1,0:T(8,128)(2,1)S(1)}, bf16[1,192,1024]{2,1,0:T(8,128)(2,1)S(1)}, u32[]{:S(2)}, u32[]{:S(2)}) %collective-permute-start) | collective-permute-done | bytes 393248 | tf_op jit(solution)/shard_map/ppermute | solution.py:14
  265.4 5.3 %collective-permute-start.1 = (bf16[1,192,1024]{2,1,0:T(8,128)(2,1)S(1)}, bf16[1,192,1024]{2,1,0:T(8,128)(2,1)S(1)}, u32[]{:S(2)}, u32[]{:S(2)}) collective-permute-start(bf16[1,192,1024]{2,1,0:T(8,128)(2,1)S(1)} %collective-permute-done), channel_id=1, source_target_pairs={{0,7},{1,0},{2,1},{3,2},{4,3},{5,4},{6,5},{7,6},{8,15},{9,8},{10,9... | collective-permute-start | bytes 1179656 | tf_op jit(solution)/shard_map/ppermute | solution.py:14
  270.7 5.3 %collective-permute-done.1 = bf16[1,192,1024]{2,1,0:T(8,128)(2,1)S(1)} collective-permute-done((bf16[1,192,1024]{2,1,0:T(8,128)(2,1)S(1)}, bf16[1,192,1024]{2,1,0:T(8,128)(2,1)S(1)}, u32[]{:S(2)}, u32[]{:S(2)}) %collective-permute-start.1) | collective-permute-done | bytes 393248 | tf_op jit(solution)/shard_map/ppermute | solution.py:14
  276.1 5.3 %collective-permute-start.2 = (bf16[1,192,1024]{2,1,0:T(8,128)(2,1)S(1)}, bf16[1,192,1024]{2,1,0:T(8,128)(2,1)S(1)}, u32[]{:S(2)}, u32[]{:S(2)}) collective-permute-start(bf16[1,192,1024]{2,1,0:T(8,128)(2,1)S(1)} %collective-permute-done.1), channel_id=1, source_target_pairs={{0,7},{1,0},{2,1},{3,2},{4,3},{5,4},{6,5},{7,6},{8,15},{9,8},{10,9... | collective-permute-start | bytes 1179656 | tf_op jit(solution)/shard_map/ppermute | solution.py:14
  281.4 4.7 %collective-permute-done.2 = bf16[1,192,1024]{2,1,0:T(8,128)(2,1)S(1)} collective-permute-done((bf16[1,192,1024]{2,1,0:T(8,128)(2,1)S(1)}, bf16[1,192,1024]{2,1,0:T(8,128)(2,1)S(1)}, u32[]{:S(2)}, u32[]{:S(2)}) %collective-permute-start.2) | collective-permute-done | bytes 393248 | tf_op jit(solution)/shard_map/ppermute | solution.py:14
  286.1 5.0 %collective-permute-start.3 = (bf16[1,192,1024]{2,1,0:T(8,128)(2,1)S(1)}, bf16[1,192,1024]{2,1,0:T(8,128)(2,1)S(1)}, u32[]{:S(2)}, u32[]{:S(2)}) collective-permute-start(bf16[1,192,1024]{2,1,0:T(8,128)(2,1)S(1)} %collective-permute-done.2), channel_id=1, source_target_pairs={{0,7},{1,0},{2,1},{3,2},{4,3},{5,4},{6,5},{7,6},{8,15},{9,8},{10,9... | collective-permute-start | bytes 1179656 | tf_op jit(solution)/shard_map/ppermute | solution.py:14
  291.7 4.1 %collective-permute-done.3 = bf16[1,192,1024]{2,1,0:T(8,128)(2,1)S(1)} collective-permute-done((bf16[1,192,1024]{2,1,0:T(8,128)(2,1)S(1)}, bf16[1,192,1024]{2,1,0:T(8,128)(2,1)S(1)}, u32[]{:S(2)}, u32[]{:S(2)}) %collective-permute-start.3) | collective-permute-done | bytes 393248 | tf_op jit(solution)/shard_map/ppermute | solution.py:14
  295.8 5.0 %collective-permute-start.4 = (bf16[1,192,1024]{2,1,0:T(8,128)(2,1)S(1)}, bf16[1,192,1024]{2,1,0:T(8,128)(2,1)S(1)}, u32[]{:S(2)}, u32[]{:S(2)}) collective-permute-start(bf16[1,192,1024]{2,1,0:T(8,128)(2,1)S(1)} %collective-permute-done.3), channel_id=1, source_target_pairs={{0,7},{1,0},{2,1},{3,2},{4,3},{5,4},{6,5},{7,6},{8,15},{9,8},{10,9... | collective-permute-start | bytes 1179656 | tf_op jit(solution)/shard_map/ppermute | solution.py:14
  301.8 3.8 collective-permute-done.4
  305.6 5.0 %collective-permute-start.5 = (bf16[1,192,1024]{2,1,0:T(8,128)(2,1)S(1)}, bf16[1,192,1024]{2,1,0:T(8,128)(2,1)S(1)}, u32[]{:S(2)}, u32[]{:S(2)}) collective-permute-start(bf16[1,192,1024]{2,1,0:T(8,128)(2,1)S(1)} %collective-permute-done.4), channel_id=1, source_target_pairs={{0,7},{1,0},{2,1},{3,2},{4,3},{5,4},{6,5},{7,6},{8,15},{9,8},{10,9... | collective-permute-start | bytes 1179656 | tf_op jit(solution)/shard_map/ppermute | solution.py:14
  311.6 4.9 %collective-permute-done.5 = bf16[1,192,1024]{2,1,0:T(8,128)(2,1)S(1)} collective-permute-done((bf16[1,192,1024]{2,1,0:T(8,128)(2,1)S(1)}, bf16[1,192,1024]{2,1,0:T(8,128)(2,1)S(1)}, u32[]{:S(2)}, u32[]{:S(2)}) %collective-permute-start.5) | collective-permute-done | bytes 393248 | tf_op jit(solution)/shard_map/ppermute | solution.py:14
  316.5 5.2 %collective-permute-start.6 = (bf16[1,192,1024]{2,1,0:T(8,128)(2,1)S(1)}, bf16[1,192,1024]{2,1,0:T(8,128)(2,1)S(1)}, u32[]{:S(2)}, u32[]{:S(2)}) collective-permute-start(bf16[1,192,1024]{2,1,0:T(8,128)(2,1)S(1)} %collective-permute-done.5), channel_id=1, source_target_pairs={{0,7},{1,0},{2,1},{3,2},{4,3},{5,4},{6,5},{7,6},{8,15},{9,8},{10,9... | collective-permute-start | bytes 1179656 | tf_op jit(solution)/shard_map/ppermute | solution.py:14
  322.7 5.8 %collective-permute-done.6 = bf16[1,192,1024]{2,1,0:T(8,128)(2,1)S(1)} collective-permute-done((bf16[1,192,1024]{2,1,0:T(8,128)(2,1)S(1)}, bf16[1,192,1024]{2,1,0:T(8,128)(2,1)S(1)}, u32[]{:S(2)}, u32[]{:S(2)}) %collective-permute-start.6) | collective-permute-done | bytes 393248 | tf_op jit(solution)/shard_map/ppermute | solution.py:14
  329.3 3.0 copy.31
  332.8 8.0 %reduce.2 = bf16[1024,512]{1,0:T(8,128)(2,1)S(1)} reduce(bf16[1024,1,512]{2,1,0:T(2,128)(2,1)} %bitcast.112, bf16[]{:T(256)} %broadcast.136), dimensions={1}, to_apply=%bitcast.106.reduce_sub_computation | reduce | bytes 2097154
  342.4 18.3 %all-to-all-start.1 = ((bf16[64,2,4096]{2,1,0:T(2,128)(2,1)}), bf16[64,2,4096]{2,1,0:T(2,128)(2,1)S(1)}, u32[]{:S(2)}, u32[]{:S(2)}) async-start(bf16[64,2,4096]{2,1,0:T(2,128)(2,1)} %reshape.239), calls=%async_computation.1 | async-start | bytes 2097152 | tf_op jit(solution)/shard_map/all_to_all | solution.py:56
  360.9 27.9 %all-to-all-done.1 = bf16[64,2,4096]{2,1,0:T(2,128)(2,1)S(1)} async-done(((bf16[64,2,4096]{2,1,0:T(2,128)(2,1)}), bf16[64,2,4096]{2,1,0:T(2,128)(2,1)S(1)}, u32[]{:S(2)}, u32[]{:S(2)}) %all-to-all-start.1) | async-done | bytes 1048608 | tf_op jit(solution)/shard_map/all_to_all | solution.py:56
  388.8 3.5 reshape.240
  (39 shorter events, 17.7 us)
Async XLA Ops:
  0.0 291.2 %copy-start = (bf16[1,1536,512]{2,1,0:T(8,128)(2,1)S(1)}, bf16[1,1536,512]{2,1,0:T(8,128)(2,1)}, u32[]{:S(2)}) copy-start(bf16[1,1536,512]{2,1,0:T(8,128)(2,1)} %param.11) | copy-start | bytes 4718596
  47.5 201.1 %copy-start.2 = (bf16[1,192,4096]{2,1,0:T(8,128)(2,1)S(1)}, bf16[1,192,4096]{2,1,0:T(8,128)(2,1)}, u32[]{:S(2)}) copy-start(bf16[1,192,4096]{2,1,0:T(8,128)(2,1)} %param.9) | copy-start | bytes 4718596
  248.7 2.9 copy-start.3
  254.5 10.9 %collective-permute-start = (bf16[1,192,1024]{2,1,0:T(8,128)(2,1)S(1)}, bf16[1,192,1024]{2,1,0:T(8,128)(2,1)S(1)}, u32[]{:S(2)}, u32[]{:S(2)}) collective-permute-start(bf16[1,192,1024]{2,1,0:T(8,128)(2,1)S(1)} %bitcast.113), channel_id=1, source_target_pairs={{0,7},{1,0},{2,1},{3,2},{4,3},{5,4},{6,5},{7,6},{8,15},{9,8},{10,9... | collective-permute-start | bytes 1179656 | tf_op jit(solution)/shard_map/ppermute | solution.py:14
  265.4 10.6 %collective-permute-start.1 = (bf16[1,192,1024]{2,1,0:T(8,128)(2,1)S(1)}, bf16[1,192,1024]{2,1,0:T(8,128)(2,1)S(1)}, u32[]{:S(2)}, u32[]{:S(2)}) collective-permute-start(bf16[1,192,1024]{2,1,0:T(8,128)(2,1)S(1)} %collective-permute-done), channel_id=1, source_target_pairs={{0,7},{1,0},{2,1},{3,2},{4,3},{5,4},{6,5},{7,6},{8,15},{9,8},{10,9... | collective-permute-start | bytes 1179656 | tf_op jit(solution)/shard_map/ppermute | solution.py:14
  276.1 10.0 %collective-permute-start.2 = (bf16[1,192,1024]{2,1,0:T(8,128)(2,1)S(1)}, bf16[1,192,1024]{2,1,0:T(8,128)(2,1)S(1)}, u32[]{:S(2)}, u32[]{:S(2)}) collective-permute-start(bf16[1,192,1024]{2,1,0:T(8,128)(2,1)S(1)} %collective-permute-done.1), channel_id=1, source_target_pairs={{0,7},{1,0},{2,1},{3,2},{4,3},{5,4},{6,5},{7,6},{8,15},{9,8},{10,9... | collective-permute-start | bytes 1179656 | tf_op jit(solution)/shard_map/ppermute | solution.py:14
  286.1 9.7 %collective-permute-start.3 = (bf16[1,192,1024]{2,1,0:T(8,128)(2,1)S(1)}, bf16[1,192,1024]{2,1,0:T(8,128)(2,1)S(1)}, u32[]{:S(2)}, u32[]{:S(2)}) collective-permute-start(bf16[1,192,1024]{2,1,0:T(8,128)(2,1)S(1)} %collective-permute-done.2), channel_id=1, source_target_pairs={{0,7},{1,0},{2,1},{3,2},{4,3},{5,4},{6,5},{7,6},{8,15},{9,8},{10,9... | collective-permute-start | bytes 1179656 | tf_op jit(solution)/shard_map/ppermute | solution.py:14
  295.8 9.8 %collective-permute-start.4 = (bf16[1,192,1024]{2,1,0:T(8,128)(2,1)S(1)}, bf16[1,192,1024]{2,1,0:T(8,128)(2,1)S(1)}, u32[]{:S(2)}, u32[]{:S(2)}) collective-permute-start(bf16[1,192,1024]{2,1,0:T(8,128)(2,1)S(1)} %collective-permute-done.3), channel_id=1, source_target_pairs={{0,7},{1,0},{2,1},{3,2},{4,3},{5,4},{6,5},{7,6},{8,15},{9,8},{10,9... | collective-permute-start | bytes 1179656 | tf_op jit(solution)/shard_map/ppermute | solution.py:14
  305.6 10.9 %collective-permute-start.5 = (bf16[1,192,1024]{2,1,0:T(8,128)(2,1)S(1)}, bf16[1,192,1024]{2,1,0:T(8,128)(2,1)S(1)}, u32[]{:S(2)}, u32[]{:S(2)}) collective-permute-start(bf16[1,192,1024]{2,1,0:T(8,128)(2,1)S(1)} %collective-permute-done.4), channel_id=1, source_target_pairs={{0,7},{1,0},{2,1},{3,2},{4,3},{5,4},{6,5},{7,6},{8,15},{9,8},{10,9... | collective-permute-start | bytes 1179656 | tf_op jit(solution)/shard_map/ppermute | solution.py:14
  316.5 12.0 %collective-permute-start.6 = (bf16[1,192,1024]{2,1,0:T(8,128)(2,1)S(1)}, bf16[1,192,1024]{2,1,0:T(8,128)(2,1)S(1)}, u32[]{:S(2)}, u32[]{:S(2)}) collective-permute-start(bf16[1,192,1024]{2,1,0:T(8,128)(2,1)S(1)} %collective-permute-done.5), channel_id=1, source_target_pairs={{0,7},{1,0},{2,1},{3,2},{4,3},{5,4},{6,5},{7,6},{8,15},{9,8},{10,9... | collective-permute-start | bytes 1179656 | tf_op jit(solution)/shard_map/ppermute | solution.py:14
  340.8 20.0 %copy-start.1 = (f32[64,8]{0,1:T(8,128)S(1)}, f32[64,8]{0,1:T(8,128)}, u32[]{:S(2)}) copy-start(f32[64,8]{0,1:T(8,128)} %param.8) | copy-start | bytes 6148
  342.4 46.3 %all-to-all-start.1 = ((bf16[64,2,4096]{2,1,0:T(2,128)(2,1)}), bf16[64,2,4096]{2,1,0:T(2,128)(2,1)S(1)}, u32[]{:S(2)}, u32[]{:S(2)}) async-start(bf16[64,2,4096]{2,1,0:T(2,128)(2,1)} %reshape.239), calls=%async_computation.1 | async-start | bytes 2097152 | tf_op jit(solution)/shard_map/all_to_all | solution.py:56
